TPU v7x, 256 devices: a whole 4x4x8 slice. The times are simulated.
256 devices in a mesh: expert: 32 (over y, z_lo, x), replica: 8 (over z_hi, core).
Axes of the slice: x: 4, y: 4, z: 8 (z_hi: 4, z_lo: 2; z = z_hi * 2 + z_lo), core: 2. Of those that a mesh axis runs over, the one named last changes fastest.
Arguments:
- tokens: bfloat16 [4096, 4096], P('expert', 'replica'), may hold values from -6 to 6
- out_grad: bfloat16 [4096, 4096], P('expert', 'replica'), may hold values from -6 to 6
- expert_ids: int32 [4096, 8], P('expert'), may hold values from 0 to 63, all different within a row; in each aligned block of 128 rows (0 to 127, 128 to 255, ...) at most 20 rows name the same one
- route_weight: float32 [4096, 8], P('expert'), may hold values from 0.05 to 0.3
- gate_weight: bfloat16 [64, 4096, 768], P('expert', 'replica'), may hold values from -0.09375 to 0.09375
- up_weight: bfloat16 [64, 4096, 768], P('expert', 'replica'), may hold values from -0.09375 to 0.09375
- down_weight: bfloat16 [64, 768, 4096], P('expert', None, 'replica'), may hold values from -0.21875 to 0.21875
Outputs:
- mixed: bfloat16 [4096, 4096], P('expert', 'replica')
- in_grad: bfloat16 [4096, 4096], P('expert', 'replica')
- grad_gate: bfloat16 [64, 4096, 768], P('expert', 'replica')
- grad_up: bfloat16 [64, 4096, 768], P('expert', 'replica')
- grad_down: bfloat16 [64, 768, 4096], P('expert', None, 'replica')
Inputs may be any that keep to these rules, and one draw needn't show every extreme that they name: `expert_ids`: each token names 8 different experts. Within the 128 rows of one index of expert no expert is named more than 20 times, a bound that some block reaches.
All inputs are finite; a program needn't handle non-finite values.
Results may differ from a plain program's by a relative error of at most 0.0064.
Values may be sent and summed in bfloat16 or wider, within the bound.
No kernel may reach another device: no remote copies, remote signals or barrier semaphores. Data moves between devices by JAX's collectives and lax.ppermute only.
A program may use at most 128 MiB of HBM per device.

v0:
```python
import jax
import jax.numpy as jnp
from jax import lax
from jax.sharding import PartitionSpec as P


def local(tokens, out_grad, expert_ids, route_weight, gate_weight, up_weight, down_weight):
    n_cols = lax.axis_size("expert")
    n_reps = lax.axis_size("replica")
    tok_count, topk = expert_ids.shape
    local_experts = gate_weight.shape[0]
    width = gate_weight.shape[2]
    experts_all = local_experts * n_cols
    capacity = tok_count * topk * 5 // (4 * experts_all)
    slots = experts_all * capacity
    share_rows = n_cols // n_reps
    flat_ids = expert_ids.reshape(-1)
    onehot = (flat_ids[:, None] == jnp.arange(experts_all, dtype=jnp.int32)[None, :]).astype(
        jnp.int32
    )
    ranks = jnp.sum((jnp.cumsum(onehot, axis=0) - 1) * onehot, axis=1)
    target = flat_ids * capacity + ranks
    place = (target[:, None] == jnp.arange(slots, dtype=jnp.int32)[None, :]).astype(jnp.float32)
    slot_weight = jnp.sum(place * route_weight.reshape(-1)[:, None], axis=0)
    place = place.reshape(tok_count, topk, slots)
    picker = jnp.sum(place, axis=1).astype(jnp.bfloat16)
    feats = tokens.shape[1]
    send_x = lax.dot_general(
        picker, tokens, (((0,), (0,)), ((), ())), preferred_element_type=jnp.float32
    ).astype(jnp.bfloat16)
    picked_g = lax.dot_general(
        picker, out_grad, (((0,), (0,)), ((), ())), preferred_element_type=jnp.float32
    )
    send_g = (slot_weight[:, None] * picked_g).astype(jnp.bfloat16)
    send_x = send_x.reshape(n_cols, local_experts, capacity, feats)
    send_g = send_g.reshape(n_cols, local_experts, capacity, feats)
    recv_x = lax.all_to_all(send_x, "expert", split_axis=0, concat_axis=0, tiled=True)
    replica_index = lax.axis_index("replica")
    piece = recv_x
    gate_part = jnp.einsum("jecd,edh->jech", piece, gate_weight, preferred_element_type=jnp.float32)
    up_part = jnp.einsum("jecd,edh->jech", piece, up_weight, preferred_element_type=jnp.float32)
    summed = lax.psum(jnp.concatenate([gate_part, up_part], axis=3), "replica")
    gate_all = summed[..., :width]
    hidden = (jax.nn.silu(gate_all) * summed[..., width:]).astype(jnp.bfloat16)
    share = lax.dynamic_slice_in_dim(summed, replica_index * share_rows, share_rows, 0)
    gate_share = share[..., :width]
    up_share = share[..., width:]
    expert_out = jnp.einsum(
        "jech,ehd->jecd", hidden, down_weight, preferred_element_type=jnp.float32
    ).astype(jnp.bfloat16)
    returned = lax.all_to_all(expert_out, "expert", split_axis=0, concat_axis=0, tiled=True)
    chosen_rows = jnp.take(returned.reshape(slots, feats), target, axis=0).astype(jnp.float32)
    chosen_rows = chosen_rows.reshape(tok_count, topk, feats)
    mixed = jnp.sum(route_weight[:, :, None] * chosen_rows, axis=1).astype(jnp.bfloat16)
    recv_g = lax.all_to_all(send_g, "expert", split_axis=0, concat_axis=0, tiled=True)
    grad_down = jnp.einsum(
        "jech,jecd->ehd", hidden, recv_g, preferred_element_type=jnp.float32
    ).astype(jnp.bfloat16)
    piece = recv_g
    hidden_grad = lax.psum_scatter(
        jnp.einsum("jecd,ehd->jech", piece, down_weight, preferred_element_type=jnp.float32),
        "replica",
        scatter_dimension=0,
        tiled=True,
    )
    sig = jax.nn.sigmoid(gate_share)
    act = gate_share * sig
    gate_grad = (hidden_grad * up_share * sig * (1.0 + gate_share * (1.0 - sig))).astype(
        jnp.bfloat16
    )
    up_grad = (hidden_grad * act).astype(jnp.bfloat16)
    both_grads = lax.all_gather(
        jnp.concatenate([gate_grad, up_grad], axis=3), "replica", axis=0, tiled=True
    )
    gate_all_grad = both_grads[..., :width]
    up_all_grad = both_grads[..., width:]
    grad_gate = jnp.einsum(
        "jecd,jech->edh", recv_x, gate_all_grad, preferred_element_type=jnp.float32
    ).astype(jnp.bfloat16)
    grad_up = jnp.einsum(
        "jecd,jech->edh", recv_x, up_all_grad, preferred_element_type=jnp.float32
    ).astype(jnp.bfloat16)
    slot_in = (
        jnp.einsum("jech,edh->jecd", gate_all_grad, gate_weight, preferred_element_type=jnp.float32)
        + jnp.einsum("jech,edh->jecd", up_all_grad, up_weight, preferred_element_type=jnp.float32)
    ).astype(jnp.bfloat16)
    back_in = lax.all_to_all(slot_in, "expert", split_axis=0, concat_axis=0, tiled=True)
    in_grad = jnp.dot(
        picker, back_in.reshape(slots, feats), preferred_element_type=jnp.float32
    ).astype(jnp.bfloat16)
    return (mixed, in_grad, grad_gate, grad_up, grad_down)


def solution(mesh):
    in_specs = (
        P("expert", "replica"),
        P("expert", "replica"),
        P("expert", None),
        P("expert", None),
        P("expert", "replica", None),
        P("expert", "replica", None),
        P("expert", None, "replica"),
    )
    out_specs = (
        P("expert", "replica"),
        P("expert", "replica"),
        P("expert", "replica", None),
        P("expert", "replica", None),
        P("expert", None, "replica"),
    )
    return jax.shard_map(local, mesh=mesh, in_specs=in_specs, out_specs=out_specs, check_vma=False)
```

profile of v0, /device:TPU:1, one launch (start us, length us, event | category | flops | bytes accessed | tf_op | source)
XLA Modules:
  0.0 471.5 jit_solution(4206737577058164144)
XLA Ops:
  7.2 0.9 copy.93
  8.1 0.1 eq.46
  8.2 0.1 reshape.104
  8.3 18.0 %reduce-window.6 = s32[64,8,128]{2,1,0:T(8,128)S(1)} reduce-window(s32[64,8,128]{2,1,0:T(8,128)S(1)} %fusion.37, s32[]{:T(128)} %constant.16.clone.1), window={size=1x1x128 pad=0_0x0_0x127_0}, to_apply=%region_0.0 | reduce-window | flops 8323072 | bytes 524292 | tf_op jit(solution)/shard_map/reduce-window
  26.3 0.1 slice.34
  26.5 0.1 copy.95
  26.7 0.1 copy.96
  26.7 0.1 add_add_fusion
  26.9 0.1 fusion.36
  27.0 0.1 reduce_sum.41
  27.1 0.1 copy.99
  27.2 1.6 convert_reduce_fusion
  28.9 0.5 convolution_convert_fusion
  29.4 1.3 reshape.106
  30.7 3.5 copy.100
  34.2 9.3 %all-to-all-start = ((bf16[32,2,20,512]{3,1,2,0:T(2,128)(2,1)}), bf16[32,2,20,512]{3,1,2,0:T(2,128)(2,1)S(1)}, u32[]{:S(2)}, u32[]{:S(2)}) async-start(bf16[32,2,20,512]{3,1,2,0:T(2,128)(2,1)} %copy.100), calls=%async_computation | async-start | bytes 2621440 | tf_op jit(solution)/shard_map/all_to_all | solution.py:37
  43.5 0.1 copy.92
  43.6 0.1 mul.94
  43.7 0.7 select_reduce_fusion
  44.4 1.6 fusion.1
  46.0 3.2 reshape.108
  49.2 3.5 copy.107
  52.7 9.0 %all-to-all-done = bf16[32,2,20,512]{3,1,2,0:T(2,128)(2,1)S(1)} async-done(((bf16[32,2,20,512]{3,1,2,0:T(2,128)(2,1)}), bf16[32,2,20,512]{3,1,2,0:T(2,128)(2,1)S(1)}, u32[]{:S(2)}, u32[]{:S(2)}) %all-to-all-start) | async-done | bytes 1310752 | tf_op jit(solution)/shard_map/all_to_all | solution.py:37
  61.7 6.4 %all-to-all-start.2 = ((bf16[32,2,20,512]{3,1,2,0:T(2,128)(2,1)}), bf16[32,2,20,512]{3,1,2,0:T(2,128)(2,1)}, u32[]{:S(2)}, u32[]{:S(2)}) async-start(bf16[32,2,20,512]{3,1,2,0:T(2,128)(2,1)} %copy.107), calls=%async_computation.2 | async-start | bytes 2621440 | tf_op jit(solution)/shard_map/all_to_all | solution.py:55
  68.1 0.2 all-reduce.4.cloned.1.call-start
  68.3 2.9 convolution_bitcast_fusion.1
  71.2 1.4 convolution_bitcast_fusion.2
  72.7 4.1 pad_maximum_fusion
  76.8 8.8 %all-to-all-done.2 = bf16[32,2,20,512]{3,1,2,0:T(2,128)(2,1)} async-done(((bf16[32,2,20,512]{3,1,2,0:T(2,128)(2,1)}), bf16[32,2,20,512]{3,1,2,0:T(2,128)(2,1)}, u32[]{:S(2)}, u32[]{:S(2)}) %all-to-all-start.2) | async-done | bytes 1310752 | tf_op jit(solution)/shard_map/all_to_all | solution.py:55
  85.6 4.7 convolution_bitcast_fusion
  90.3 0.0 all-gather.2.cloned.1.call-start
  90.3 0.6 copy-done.13
  90.9 0.6 dynamic-slice
  92.2 254.9 %all-reduce.4.cloned.1.call-done = (f32[32,2,20,1536]{3,0,2,1:T(8,128)}, f32[32,2,20,768]{3,0,2,1:T(8,128)}) async-done(((f32[32,2,20,1536]{3,0,2,1:T(8,128)}, f32[32,2,20,768]{3,0,2,1:T(8,128)}), (f32[32,2,20,1536]{3,0,2,1:T(8,128)}, f32[32,2,20,768]{3,0,2,1:T(8,128)})) %all-reduce.4.cloned.1.call-update) | async-done | bytes 11796496 | tf_op jit(solution)/shard_map/psum | solution.py:42
  347.1 2.5 fusion.34
  349.5 0.2 pad_maximum_fusion.1
  349.8 1.3 copy.109
  351.1 4.5 fusion
  355.6 1.2 fusion.18
  356.8 0.1 copy-done.6
  356.9 2.4 copy.103
  359.3 8.5 %all-to-all-start.1 = ((bf16[32,2,20,512]{3,1,2,0:T(2,128)(2,1)}), bf16[32,2,20,512]{3,1,2,0:T(2,128)(2,1)}, u32[]{:S(2)}, u32[]{:S(2)}) async-start(bf16[32,2,20,512]{3,1,2,0:T(2,128)(2,1)} %copy.103), calls=%async_computation.1 | async-start | bytes 2621440 | tf_op jit(solution)/shard_map/all_to_all | solution.py:51
  367.9 0.1 copy.105
  368.0 0.1 mul.90
  368.1 0.1 copy.98
  368.2 46.5 %all-gather.2.cloned.1.call-done = bf16[32,2,20,1536]{3,1,2,0:T(2,128)(2,1)} async-done(((bf16[4,2,20,1536]{3,1,2,0:T(2,128)(2,1)}), bf16[32,2,20,1536]{3,1,2,0:T(2,128)(2,1)}) %all-gather.2.cloned.1.call-update) | async-done | bytes 3932176 | tf_op jit(solution)/shard_map/all_gather | solution.py:72
  414.7 4.6 fusion.43
  419.4 1.2 fusion.3
  420.6 0.0 copy-done.7
  420.6 0.6 copy-done.2
  421.2 0.7 copy-done.5
  421.9 1.2 fusion.21
  423.2 2.5 copy.112
  425.7 7.0 %all-to-all-start.3 = ((bf16[32,2,20,512]{3,1,2,0:T(2,128)(2,1)}), bf16[32,2,20,512]{3,1,2,0:T(2,128)(2,1)}, u32[]{:S(2)}, u32[]{:S(2)}) async-start(bf16[32,2,20,512]{3,1,2,0:T(2,128)(2,1)} %copy.112), calls=%async_computation.3 | async-start | bytes 2621440 | tf_op jit(solution)/shard_map/all_to_all | solution.py:87
  432.6 4.6 bitcast_convert_fusion
  437.2 2.8 copy.104
  440.0 2.3 reshape.107
  442.3 5.1 %gather_fusion = bf16[1024,512]{1,0:T(8,128)(2,1)} fusion(bf16[1280,512]{1,0:T(8,128)(2,1)S(1)} %reshape.107, s32[1024]{0:T(1024)S(1)} %broadcast_clamp_fusion), kind=kCustom, calls=%fused_computation | custom fusion | bytes 2101248 | tf_op jit(solution)/shard_map/jit(_take)/gather | solution.py:52
  447.4 2.7 multiply_reduce_fusion
  450.0 5.0 %bitcast_convert_fusion.1 = bf16[2,512,768]{2,1,0:T(8,128)(2,1)} fusion(bf16[32,2,20,768]{3,1,2,0:T(2,128)(2,1)} %copy-done.7, bf16[32,2,20,512]{3,1,2,0:T(2,128)(2,1)S(1)} %all-to-all-done), kind=kOutput, calls=%fused_computation.10 | convolution fusion | flops 1007419392 | bytes 4849664 | tf_op jit(solution)/shard_map/jecd,jech->edh/dot_general | solution.py:80
  455.0 3.3 bitcast_convert_fusion.2
  458.4 2.9 copy.113
  461.3 2.3 reshape.109
  463.6 1.0 convolution_convert_fusion.2
  (36 shorter events, 0.2 us)
Async XLA Ops:
  7.2 78.4 %copy-start = (bf16[2,768,512]{2,1,0:T(8,128)(2,1)S(1)}, bf16[2,768,512]{2,1,0:T(8,128)(2,1)}, u32[]{:S(2)}) copy-start(bf16[2,768,512]{2,1,0:T(8,128)(2,1)} %param.13) | copy-start | bytes 4718596
  7.2 19.9 %copy-start.11 = (s32[128,8]{0,1:T(8,128)S(1)}, s32[128,8]{0,1:T(8,128)}, u32[]{:S(2)}) copy-start(s32[128,8]{0,1:T(8,128)} %param.9) | copy-start | bytes 12292
  7.2 21.7 %copy-start.9 = (bf16[128,512]{1,0:T(8,128)(2,1)S(1)}, bf16[128,512]{1,0:T(8,128)(2,1)}, u32[]{:S(2)}) copy-start(bf16[128,512]{1,0:T(8,128)(2,1)} %param.7) | copy-start | bytes 393220
  34.1 9.4 %copy-start.12 = (f32[128,8]{0,1:T(8,128)S(1)}, f32[128,8]{0,1:T(8,128)}, u32[]{:S(2)}) copy-start(f32[128,8]{0,1:T(8,128)} %param.10) | copy-start | bytes 12292
  34.1 10.2 %copy-start.10 = (bf16[128,512]{1,0:T(8,128)(2,1)S(1)}, bf16[128,512]{1,0:T(8,128)(2,1)}, u32[]{:S(2)}) copy-start(bf16[128,512]{1,0:T(8,128)(2,1)} %param.8) | copy-start | bytes 393220
  34.2 27.5 %all-to-all-start = ((bf16[32,2,20,512]{3,1,2,0:T(2,128)(2,1)}), bf16[32,2,20,512]{3,1,2,0:T(2,128)(2,1)S(1)}, u32[]{:S(2)}, u32[]{:S(2)}) async-start(bf16[32,2,20,512]{3,1,2,0:T(2,128)(2,1)} %copy.100), calls=%async_computation | async-start | bytes 2621440 | tf_op jit(solution)/shard_map/all_to_all | solution.py:37
  61.7 23.9 %all-to-all-start.2 = ((bf16[32,2,20,512]{3,1,2,0:T(2,128)(2,1)}), bf16[32,2,20,512]{3,1,2,0:T(2,128)(2,1)}, u32[]{:S(2)}, u32[]{:S(2)}) async-start(bf16[32,2,20,512]{3,1,2,0:T(2,128)(2,1)} %copy.107), calls=%async_computation.2 | async-start | bytes 2621440 | tf_op jit(solution)/shard_map/all_to_all | solution.py:55
  68.1 279.0 %all-reduce.4.cloned.1.call-start = ((), (), s32[]{:S(2)}) async-start(), calls=%async_computation.5 | async-start | bytes 23592960 | tf_op jit(solution)/shard_map/psum | solution.py:42
  68.3 2.9 copy-start.4
  90.3 0.7 copy-start.13
  90.3 324.4 %all-gather.2.cloned.1.call-start = ((), (), s32[]{:S(2)}) async-start(), calls=%async_computation.4 | async-start | bytes 4423680 | tf_op jit(solution)/shard_map/all_gather | solution.py:72
  355.6 1.3 copy-start.6
  359.3 66.4 %all-to-all-start.1 = ((bf16[32,2,20,512]{3,1,2,0:T(2,128)(2,1)}), bf16[32,2,20,512]{3,1,2,0:T(2,128)(2,1)}, u32[]{:S(2)}, u32[]{:S(2)}) async-start(bf16[32,2,20,512]{3,1,2,0:T(2,128)(2,1)} %copy.103), calls=%async_computation.1 | async-start | bytes 2621440 | tf_op jit(solution)/shard_map/all_to_all | solution.py:51
  414.7 4.6 copy-start.8
  419.3 1.3 copy-start.7
  419.3 1.9 copy-start.2
  419.3 2.6 copy-start.5
  425.7 32.7 %all-to-all-start.3 = ((bf16[32,2,20,512]{3,1,2,0:T(2,128)(2,1)}), bf16[32,2,20,512]{3,1,2,0:T(2,128)(2,1)}, u32[]{:S(2)}, u32[]{:S(2)}) async-start(bf16[32,2,20,512]{3,1,2,0:T(2,128)(2,1)} %copy.112), calls=%async_computation.3 | async-start | bytes 2621440 | tf_op jit(solution)/shard_map/all_to_all | solution.py:87
  450.0 5.0 %copy-start.3 = (bf16[32,2,20,768]{3,1,2,0:T(2,128)(2,1)S(1)}, bf16[32,2,20,768]{3,1,2,0:T(2,128)(2,1)}, u32[]{:S(2)}) copy-start(bf16[32,2,20,768]{3,1,2,0:T(2,128)(2,1)} %copy-done.2) | copy-start | bytes 5898244
  458.4 6.2 %copy-start.1 = (bf16[2,768,512]{2,1,0:T(8,128)(2,1)S(1)}, bf16[2,768,512]{2,1,0:T(8,128)(2,1)}, u32[]{:S(2)}) copy-start(bf16[2,768,512]{2,1,0:T(8,128)(2,1)} %param.13) | copy-start | bytes 4718596
Sparse Core Ops, SparseCore 0:
  90.4 256.6 all-reduce.3
  351.2 63.4 all-gather.1
where the time goes:
time: 472 us; the launch traced here: 471 us
  waiting for transfers between devices  319 us (68%)
  local copies, waits for them, and re-layouts  42.4 us (9%)
  other arithmetic  34.6 us (7%)
  starting transfers between devices  31.5 us (7%)
  matrix products  28.7 us (6%)
  between operations  15 us (3%)
    psum x1, waiting for transfers between devices, local(): summed = lax.psum(jnp.concatenate([gate_part, up_part], axis=3), 'replica')  255 us
    all_gather x1, waiting for transfers between devices, local(): lax.all_gather(jnp.concatenate([gate_grad, up_grad], axis=3), 'replica',...  46.5 us
    another operation x2, other arithmetic  18 us
  transfers between devices with their start and end apart: 6, of which 4 were waited for; matrix products, arithmetic and copies ran while one was open for 13% of the time, Pallas kernels for 0%

commit v1 on v0

--- a/solution.py
+++ b/solution.py
@@ -2,6 +2,7 @@
 import jax.numpy as jnp
 from jax import lax
 from jax.sharding import PartitionSpec as P
+from jax.lax import all_to_all, axis_size
 
 
 def local(tokens, out_grad, expert_ids, route_weight, gate_weight, up_weight, down_weight):
@@ -69,8 +70,14 @@
         jnp.bfloat16
     )
     up_grad = (hidden_grad * act).astype(jnp.bfloat16)
-    both_grads = lax.all_gather(
-        jnp.concatenate([gate_grad, up_grad], axis=3), "replica", axis=0, tiled=True
+    both_grads = jnp.concatenate(
+        all_to_all(
+            jnp.stack([jnp.concatenate([gate_grad, up_grad], axis=3)] * axis_size("replica")),
+            axis_name="replica",
+            split_axis=0,
+            concat_axis=0,
+        ),
+        axis=0,
     )
     gate_all_grad = both_grads[..., :width]
     up_all_grad = both_grads[..., width:]

time: 472 us -> 524 us (1.11)
  starting transfers between devices: 31.5 us -> 51.9 us
  waiting for transfers between devices: 319 us -> 336 us
  local copies, waits for them, and re-layouts: 42.4 us -> 52.1 us
    all_to_all x0 -> x1, waiting for transfers between devices: none -> 63.5 us  [local(): all_to_all(jnp.stack([jnp.concatenate([gate_grad, up_grad], axis=3)] * ax...]
    all_gather x1 -> x0, waiting for transfers between devices: 46.5 us -> none  [local(): lax.all_gather(jnp.concatenate([gate_grad, up_grad], axis=3), 'replica',...]
    all_to_all x1, starting transfers between devices: 8.53 us -> 23.5 us  [local(): lax.all_to_all(expert_out, 'expert', split_axis=0, concat_axis=0, tiled=T...]
    reshape x0 -> x1, local copies, waits for them, and re-layouts: none -> 7.12 us  [local(): jnp.concatenate(all_to_all(jnp.stack([jnp.concatenate([gate_grad, up_grad...]
    all_to_all x0 -> x1, local copies, waits for them, and re-layouts: none -> 6.08 us  [local(): all_to_all(jnp.stack([jnp.concatenate([gate_grad, up_grad], axis=3)] * ax...]
  transfers between devices with their start and end apart: 6 -> 6, of which waited for: 4 -> 4; matrix products, arithmetic and copies ran while one was open for 13% -> 14% of each run, Pallas kernels for 0% -> 0%
where the time goes in v1:
time: 524 us; the launch traced here: 520 us
  waiting for transfers between devices  336 us (64%)
  local copies, waits for them, and re-layouts  52.1 us (10%)
  starting transfers between devices  51.9 us (10%)
  other arithmetic  34.6 us (7%)
  matrix products  30.3 us (6%)
  between operations  15 us (3%)
    psum x1, waiting for transfers between devices, local(): summed = lax.psum(jnp.concatenate([gate_part, up_part], axis=3), 'replica')  255 us
    all_to_all x1, waiting for transfers between devices, local(): all_to_all(jnp.stack([jnp.concatenate([gate_grad, up_grad], axis=3)] * ax...  63.5 us
    all_to_all x1, starting transfers between devices, local(): lax.all_to_all(expert_out, 'expert', split_axis=0, concat_axis=0, tiled=T...  23.5 us
    another operation x2, other arithmetic  18 us
  transfers between devices with their start and end apart: 6, of which 4 were waited for; matrix products, arithmetic and copies ran while one was open for 14% of the time, Pallas kernels for 0%

profile of v1, /device:TPU:1, one launch (start us, length us, event | category | flops | bytes accessed | tf_op | source)
XLA Modules:
  0.0 520.2 jit_solution(5123877012896466721)
XLA Ops:
  7.2 0.9 copy.87
  8.1 0.1 eq.46
  8.2 0.1 reshape.109
  8.3 18.0 %reduce-window.6 = s32[64,8,128]{2,1,0:T(8,128)S(1)} reduce-window(s32[64,8,128]{2,1,0:T(8,128)S(1)} %fusion.37, s32[]{:T(128)} %constant.16.clone.1), window={size=1x1x128 pad=0_0x0_0x127_0}, to_apply=%region_0.0 | reduce-window | flops 8323072 | bytes 524292 | tf_op jit(solution)/shard_map/reduce-window
  26.3 0.1 slice.34
  26.5 0.1 copy.89
  26.7 0.1 copy.90
  26.7 0.1 add_add_fusion
  26.9 0.1 fusion.36
  27.0 0.1 reduce_sum.41
  27.1 0.1 copy.93
  27.2 1.6 convert_reduce_fusion
  28.9 0.5 convolution_convert_fusion
  29.4 1.3 reshape.111
  30.7 3.5 copy.94
  34.2 9.3 %all-to-all-start = ((bf16[32,2,20,512]{3,1,2,0:T(2,128)(2,1)}), bf16[32,2,20,512]{3,1,2,0:T(2,128)(2,1)S(1)}, u32[]{:S(2)}, u32[]{:S(2)}) async-start(bf16[32,2,20,512]{3,1,2,0:T(2,128)(2,1)} %copy.94), calls=%async_computation | async-start | bytes 2621440 | tf_op jit(solution)/shard_map/all_to_all | solution.py:38
  43.5 0.1 copy.86
  43.6 0.1 mul.94
  43.7 0.7 select_reduce_fusion
  44.4 1.6 fusion.1
  46.0 3.2 reshape.113
  49.2 3.5 copy.101
  52.7 9.0 %all-to-all-done = bf16[32,2,20,512]{3,1,2,0:T(2,128)(2,1)S(1)} async-done(((bf16[32,2,20,512]{3,1,2,0:T(2,128)(2,1)}), bf16[32,2,20,512]{3,1,2,0:T(2,128)(2,1)S(1)}, u32[]{:S(2)}, u32[]{:S(2)}) %all-to-all-start) | async-done | bytes 1310752 | tf_op jit(solution)/shard_map/all_to_all | solution.py:38
  61.7 6.4 %all-to-all-start.2 = ((bf16[32,2,20,512]{3,1,2,0:T(2,128)(2,1)}), bf16[32,2,20,512]{3,1,2,0:T(2,128)(2,1)}, u32[]{:S(2)}, u32[]{:S(2)}) async-start(bf16[32,2,20,512]{3,1,2,0:T(2,128)(2,1)} %copy.101), calls=%async_computation.2 | async-start | bytes 2621440 | tf_op jit(solution)/shard_map/all_to_all | solution.py:56
  68.1 0.2 all-reduce.4.cloned.1.call-start
  68.3 2.9 convolution_bitcast_fusion.1
  71.2 1.4 convolution_bitcast_fusion.2
  72.7 4.1 pad_maximum_fusion
  76.8 8.8 %all-to-all-done.2 = bf16[32,2,20,512]{3,1,2,0:T(2,128)(2,1)} async-done(((bf16[32,2,20,512]{3,1,2,0:T(2,128)(2,1)}), bf16[32,2,20,512]{3,1,2,0:T(2,128)(2,1)}, u32[]{:S(2)}, u32[]{:S(2)}) %all-to-all-start.2) | async-done | bytes 1310752 | tf_op jit(solution)/shard_map/all_to_all | solution.py:56
  85.6 4.7 convolution_bitcast_fusion
  90.3 0.0 all-reduce.4.cloned.1.call-update
  90.3 0.6 copy-done.11
  90.9 0.6 dynamic-slice
  92.2 254.9 %all-reduce.4.cloned.1.call-done = (f32[32,2,20,1536]{3,0,2,1:T(8,128)}, f32[32,2,20,768]{3,0,2,1:T(8,128)}) async-done(((f32[32,2,20,1536]{3,0,2,1:T(8,128)}, f32[32,2,20,768]{3,0,2,1:T(8,128)}), (f32[32,2,20,1536]{3,0,2,1:T(8,128)}, f32[32,2,20,768]{3,0,2,1:T(8,128)})) %all-reduce.4.cloned.1.call-update) | async-done | bytes 11796496 | tf_op jit(solution)/shard_map/psum | solution.py:43
  347.1 2.5 fusion.34
  349.6 0.2 pad_maximum_fusion.1
  349.8 3.5 stack.2
  353.3 4.9 all-to-all-start.3
  358.2 4.5 fusion
  362.7 1.2 fusion.18
  363.9 0.1 copy-done.6
  364.0 2.4 copy.97
  366.4 63.5 %all-to-all-done.3 = bf16[8,4,2,20,1536]{4,1,3,2,0:T(4,128)(2,1)} async-done(((bf16[8,4,2,20,1536]{4,1,3,2,0:T(4,128)(2,1)}), bf16[8,4,2,20,1536]{4,1,3,2,0:T(4,128)(2,1)}, u32[]{:S(2)}, u32[]{:S(2)}) %all-to-all-start.3) | async-done | bytes 3932192 | tf_op jit(solution)/shard_map/all_to_all | solution.py:74
  429.9 23.5 %all-to-all-start.1 = ((bf16[32,2,20,512]{3,1,2,0:T(2,128)(2,1)}), bf16[32,2,20,512]{3,1,2,0:T(2,128)(2,1)}, u32[]{:S(2)}, u32[]{:S(2)}) async-start(bf16[32,2,20,512]{3,1,2,0:T(2,128)(2,1)} %copy.97), calls=%async_computation.1 | async-start | bytes 2621440 | tf_op jit(solution)/shard_map/all_to_all | solution.py:52
  453.4 0.1 copy.99
  453.5 0.1 mul.90
  453.6 0.1 copy.92
  453.8 6.1 %copy.103 = bf16[8,4,2,20,1536]{4,1,0,3,2:T(4,128)(2,1)} copy(bf16[8,4,2,20,1536]{4,1,3,2,0:T(4,128)(2,1)} %all-to-all-done.3) | data formatting | bytes 7864320 | tf_op jit(solution)/shard_map/all_to_all | solution.py:74
  459.9 7.1 %reshape.114 = bf16[32,2,20,1536]{3,0,2,1:T(8,128)(2,1)} reshape(bf16[8,4,2,20,1536]{4,1,0,3,2:T(4,128)(2,1)} %copy.103) | data formatting | bytes 7864320 | tf_op jit(solution)/shard_map/reshape | solution.py:73
  467.0 3.4 fusion.3
  470.4 0.3 copy-done.5
  470.6 1.2 fusion.21
  471.9 2.4 copy.104
  474.3 7.6 %all-to-all-start.4 = ((bf16[32,2,20,512]{3,1,2,0:T(2,128)(2,1)}), bf16[32,2,20,512]{3,1,2,0:T(2,128)(2,1)}, u32[]{:S(2)}, u32[]{:S(2)}) async-start(bf16[32,2,20,512]{3,1,2,0:T(2,128)(2,1)} %copy.104), calls=%async_computation.4 | async-start | bytes 2621440 | tf_op jit(solution)/shard_map/all_to_all | solution.py:94
  481.9 4.6 bitcast_convert_fusion
  486.5 2.8 copy.98
  489.2 2.3 reshape.112
  491.5 5.1 gather_fusion
  496.6 2.7 multiply_reduce_fusion
  499.3 4.7 bitcast_convert_fusion.1
  504.0 3.1 bitcast_convert_fusion.2
  507.2 2.8 copy.105
  510.0 2.4 reshape.115
  512.4 1.0 convolution_convert_fusion.2
  (32 shorter events, 0.2 us)
Async XLA Ops:
  7.2 78.4 %copy-start = (bf16[2,768,512]{2,1,0:T(8,128)(2,1)S(1)}, bf16[2,768,512]{2,1,0:T(8,128)(2,1)}, u32[]{:S(2)}) copy-start(bf16[2,768,512]{2,1,0:T(8,128)(2,1)} %param.13) | copy-start | bytes 4718596
  7.2 19.9 %copy-start.9 = (s32[128,8]{0,1:T(8,128)S(1)}, s32[128,8]{0,1:T(8,128)}, u32[]{:S(2)}) copy-start(s32[128,8]{0,1:T(8,128)} %param.9) | copy-start | bytes 12292
  8.2 20.7 %copy-start.7 = (bf16[128,512]{1,0:T(8,128)(2,1)S(1)}, bf16[128,512]{1,0:T(8,128)(2,1)}, u32[]{:S(2)}) copy-start(bf16[128,512]{1,0:T(8,128)(2,1)} %param.7) | copy-start | bytes 393220
  34.1 9.4 %copy-start.10 = (f32[128,8]{0,1:T(8,128)S(1)}, f32[128,8]{0,1:T(8,128)}, u32[]{:S(2)}) copy-start(f32[128,8]{0,1:T(8,128)} %param.10) | copy-start | bytes 12292
  34.1 10.2 %copy-start.8 = (bf16[128,512]{1,0:T(8,128)(2,1)S(1)}, bf16[128,512]{1,0:T(8,128)(2,1)}, u32[]{:S(2)}) copy-start(bf16[128,512]{1,0:T(8,128)(2,1)} %param.8) | copy-start | bytes 393220
  34.2 27.5 %all-to-all-start = ((bf16[32,2,20,512]{3,1,2,0:T(2,128)(2,1)}), bf16[32,2,20,512]{3,1,2,0:T(2,128)(2,1)S(1)}, u32[]{:S(2)}, u32[]{:S(2)}) async-start(bf16[32,2,20,512]{3,1,2,0:T(2,128)(2,1)} %copy.94), calls=%async_computation | async-start | bytes 2621440 | tf_op jit(solution)/shard_map/all_to_all | solution.py:38
  61.7 23.9 %all-to-all-start.2 = ((bf16[32,2,20,512]{3,1,2,0:T(2,128)(2,1)}), bf16[32,2,20,512]{3,1,2,0:T(2,128)(2,1)}, u32[]{:S(2)}, u32[]{:S(2)}) async-start(bf16[32,2,20,512]{3,1,2,0:T(2,128)(2,1)} %copy.101), calls=%async_computation.2 | async-start | bytes 2621440 | tf_op jit(solution)/shard_map/all_to_all | solution.py:56
  68.1 279.0 %all-reduce.4.cloned.1.call-start = ((), (), s32[]{:S(2)}) async-start(), calls=%async_computation.5 | async-start | bytes 23592960 | tf_op jit(solution)/shard_map/psum | solution.py:43
  68.3 2.9 copy-start.4
  90.3 0.7 copy-start.11
  353.3 76.7 %all-to-all-start.3 = ((bf16[8,4,2,20,1536]{4,1,3,2,0:T(4,128)(2,1)}), bf16[8,4,2,20,1536]{4,1,3,2,0:T(4,128)(2,1)}, u32[]{:S(2)}, u32[]{:S(2)}) async-start(bf16[8,4,2,20,1536]{4,1,3,2,0:T(4,128)(2,1)} %stack.2), calls=%async_computation.3 | async-start | bytes 7864320 | tf_op jit(solution)/shard_map/all_to_all | solution.py:74
  362.7 1.3 copy-start.6
  429.9 44.4 %all-to-all-start.1 = ((bf16[32,2,20,512]{3,1,2,0:T(2,128)(2,1)}), bf16[32,2,20,512]{3,1,2,0:T(2,128)(2,1)}, u32[]{:S(2)}, u32[]{:S(2)}) async-start(bf16[32,2,20,512]{3,1,2,0:T(2,128)(2,1)} %copy.97), calls=%async_computation.1 | async-start | bytes 2621440 | tf_op jit(solution)/shard_map/all_to_all | solution.py:52
  467.0 3.4 copy-start.2
  467.0 3.7 copy-start.5
  474.3 32.9 %all-to-all-start.4 = ((bf16[32,2,20,512]{3,1,2,0:T(2,128)(2,1)}), bf16[32,2,20,512]{3,1,2,0:T(2,128)(2,1)}, u32[]{:S(2)}, u32[]{:S(2)}) async-start(bf16[32,2,20,512]{3,1,2,0:T(2,128)(2,1)} %copy.104), calls=%async_computation.4 | async-start | bytes 2621440 | tf_op jit(solution)/shard_map/all_to_all | solution.py:94
  499.3 4.7 copy-start.3
  510.0 3.4 copy-start.1
Sparse Core Ops, SparseCore 0:
  90.4 256.6 all-reduce.3
